TPU v7x, 512 devices: a whole 4x8x8 slice. The times are simulated.
512 devices in a mesh: tok: 16 (over z, core), voc: 32 (over y, x).
Axes of the slice: x: 4, y: 8, z: 8, core: 2. Of those that a mesh axis runs over, the one named last changes fastest.
Arguments:
- hidden: bfloat16 [256, 2304], P('tok', 'voc'), may hold values from -18 to 18
- head: bfloat16 [2304, 131072], P(None, ('tok', 'voc')), as said below
- targets: int32 [256], replicated, may hold values from 0 to 131071
- probe_hidden: bfloat16 [256, 2304], P('tok', 'voc'), may hold values from -6 to 6
- probe_head: bfloat16 [2304, 131072], P(None, ('tok', 'voc')), may hold values from -0.5 to 0.5
Outputs:
- head_out: float32 [2304, 131072], P(None, ('tok', 'voc'))
- hidden_out: float32 [256, 2304], P('tok', 'voc')
Inputs may be any that keep to these rules, and one draw needn't show every extreme that they name: `head`: entries lie within 66 / sqrt(2304) in magnitude.
All inputs are finite; a program needn't handle non-finite values.
Results may differ from a plain program's by a relative error of at most 0.0075.
Values may be sent and summed in bfloat16 or wider, within the bound.
A program may use at most 64 MiB of HBM per device.

v0:
```python
import jax
import jax.numpy as jnp
from jax import lax
from jax.sharding import PartitionSpec as P

softcap_value = 30.0
zloss_weight = 0.0001


def local(hidden, head, targets, probe_hidden, probe_head):
    voc_count = lax.axis_size("voc")
    vocab_width = head.shape[1]
    stacked = jnp.stack([hidden, probe_hidden])
    features = lax.all_gather(stacked, "voc", axis=2, tiled=True)
    gathered = lax.all_gather(features, "tok", axis=1, tiled=True)
    row_hidden = gathered[0]
    row_probe = gathered[1]
    logits = jnp.dot(row_hidden, head, preferred_element_type=jnp.float32)
    tangent = jnp.dot(row_probe, head, preferred_element_type=jnp.float32) + jnp.dot(
        row_hidden, probe_head, preferred_element_type=jnp.float32
    )
    capped = jnp.tanh(logits / softcap_value)
    cap_slope = 1.0 - capped * capped
    exponent = jnp.exp(softcap_value * capped)
    cap_tangent = cap_slope * tangent
    row_total = lax.psum(jnp.sum(exponent, axis=1), ("tok", "voc"))
    probability = exponent / row_total[:, None]
    mean_tangent = lax.psum(jnp.sum(probability * cap_tangent, axis=1), ("tok", "voc"))
    factor = 1.0 + 2.0 * zloss_weight * jnp.log(row_total)
    offset = (lax.axis_index("tok") * voc_count + lax.axis_index("voc")) * vocab_width
    columns = offset + lax.iota(jnp.int32, vocab_width)
    onehot = (targets[:, None] == columns[None, :]).astype(jnp.float32)
    grad_cap = factor[:, None] * probability - onehot
    grad_tan = probability * (
        factor[:, None] * (cap_tangent - mean_tangent[:, None])
        + 2.0 * zloss_weight * mean_tangent[:, None]
    )
    slope_tan = -2.0 / softcap_value * capped * cap_slope * tangent
    dlogit = (grad_cap * cap_slope).astype(jnp.bfloat16)
    dlogit_tan = (grad_tan * cap_slope + grad_cap * slope_tan).astype(jnp.bfloat16)
    head_out = jnp.einsum(
        "krd,krv->dv", gathered, jnp.stack([dlogit_tan, dlogit]), preferred_element_type=jnp.float32
    )
    probe_part = lax.dot_general(
        dlogit, probe_head, (((1,), (1,)), ((), ())), preferred_element_type=jnp.float32
    )
    head_part = lax.dot_general(
        dlogit_tan, head, (((1,), (1,)), ((), ())), preferred_element_type=jnp.float32
    )
    summed = lax.psum_scatter(probe_part + head_part, "tok", scatter_dimension=0, tiled=True)
    hidden_out = lax.psum_scatter(summed, "voc", scatter_dimension=1, tiled=True)
    return (head_out, hidden_out)


def solution(mesh):
    return jax.shard_map(
        local,
        mesh=mesh,
        in_specs=(
            P("tok", "voc"),
            P(None, ("tok", "voc")),
            P(),
            P("tok", "voc"),
            P(None, ("tok", "voc")),
        ),
        out_specs=(P(None, ("tok", "voc")), P("tok", "voc")),
        check_vma=False,
    )
```

profile of v0, /device:TPU:2, one launch (start us, length us, event | category | flops | bytes accessed | tf_op | source)
XLA Modules:
  0.0 533.8 jit_solution(17602048826722212761)
XLA Ops:
  7.2 0.0 copy-start
  7.2 0.0 all-gather.2.cloned.1.call-start
  7.2 0.8 pad_maximum_fusion
  8.0 0.1 copy.12
  8.1 52.7 %all_gather.6 = bf16[2,16,2304]{1,0,2:T(2,128)(2,1)S(1)} all-gather(bf16[2,16,72]{1,0,2:T(2,128)(2,1)S(1)} %copy.12), channel_id=1, replica_groups=mesh['tok'=16,'voc'=32] {'voc'}, dimensions={2}, use_global_device_ids=true | all-gather | bytes 152064 | tf_op jit(solution)/shard_map/all_gather | solution.py:14
  60.8 2.2 copy.13
  63.0 0.0 all-gather.2.cloned.1.call-update
  63.0 0.0 reduce-scatter.3.cloned.1.call-start
  63.1 0.6 iota_add_fusion
  63.7 42.7 %all-gather.2.cloned.1.call-done = bf16[2,256,2304]{2,1,0:T(8,128)(2,1)} async-done(((bf16[2,16,2304]{2,1,0:T(8,128)(2,1)}), bf16[2,256,2304]{2,1,0:T(8,128)(2,1)}) %all-gather.2.cloned.1.call-update) | async-done | bytes 2359312 | tf_op jit(solution)/shard_map/all_gather | solution.py:15
  106.4 0.0 copy-done
  106.4 0.0 copy-start.1
  106.4 2.7 fusion.8
  109.1 96.8 %psum.14 = f32[256]{0:T(256)S(1)} all-reduce(f32[256]{0:T(256)S(1)} %get-tuple-element.4), channel_id=1, replica_groups=mesh['tok'=16,'voc'=32] {'tok','voc'}, use_global_device_ids=true, to_apply=%region_1.0 | all-reduce | flops 256 | bytes 2048 | tf_op jit(solution)/shard_map/psum | solution.py:26
  205.8 0.0 copy-done.1
  205.8 0.0 copy-start.4
  205.8 1.9 fusion.3
  207.7 0.0 copy-done.4
  207.8 0.0 copy-start.5
  207.8 1.8 multiply_reduce_fusion
  209.6 94.9 %psum.15 = f32[256]{0:T(256)S(1)} all-reduce(f32[256]{0:T(256)} %get-tuple-element.6), channel_id=1, replica_groups=mesh['tok'=16,'voc'=32] {'tok','voc'}, use_global_device_ids=true, to_apply=%region_3.0 | all-reduce | flops 256 | bytes 2048 | tf_op jit(solution)/shard_map/psum | solution.py:28
  304.5 0.0 copy-done.5
  304.5 1.2 add_convert_fusion
  305.7 0.0 copy-start.3
  305.8 0.0 copy-start.2
  305.8 1.9 fusion.10
  307.7 0.0 copy-done.3
  307.7 0.0 copy-done.2
  307.7 2.0 convolution_add_fusion
  309.6 0.0 reduce-scatter.3.cloned.1.call-update
  309.7 0.0 all-reduce.3.cloned.1.call-start
  309.7 1.3 dynamic-slice
  311.6 58.5 %reduce-scatter.3.cloned.1.call-done = f32[16,2304]{1,0:T(8,128)} async-done(((f32[256,2304]{1,0:T(8,128)}), f32[16,2304]{1,0:T(8,128)}) %reduce-scatter.3.cloned.1.call-update) | async-done | bytes 147472 | tf_op jit(solution)/shard_map/reduce_scatter | solution.py:50
  370.1 0.0 all-reduce.3.cloned.1.call-update
  370.1 3.2 convolution_bitcast_fusion
  373.3 152.5 %all-reduce.3.cloned.1.call-done = f32[16,2304]{1,0:T(8,128)} async-done(((f32[16,2304]{1,0:T(8,128)}), f32[16,2304]{1,0:T(8,128)}) %all-reduce.3.cloned.1.call-update) | async-done | bytes 147472
  525.9 1.4 constant_dynamic-slice_fusion
  (2 shorter events, 0.0 us)
Async XLA Ops:
  7.2 99.2 %copy-start = (bf16[2304,256]{1,0:T(8,128)(2,1)S(1)}, bf16[2304,256]{1,0:T(8,128)(2,1)}, u32[]{:S(2)}) copy-start(bf16[2304,256]{1,0:T(8,128)(2,1)} %param.6) | copy-start | bytes 3538948
  7.2 99.2 %all-gather.2.cloned.1.call-start = ((), (), s32[]{:S(2)}) async-start(), calls=%async_computation.1 | async-start | bytes 2506752 | tf_op jit(solution)/shard_map/all_gather | solution.py:15
  63.0 307.1 %reduce-scatter.3.cloned.1.call-start = ((), (), s32[]{:S(2)}) async-start(), calls=%async_computation.2 | async-start | bytes 2506752 | tf_op jit(solution)/shard_map/reduce_scatter | solution.py:50
  106.4 99.5 %copy-start.1 = (bf16[2,256,2304]{2,1,0:T(8,128)(2,1)S(1)}, bf16[2,256,2304]{2,1,0:T(8,128)(2,1)}, u32[]{:S(2)}) copy-start(bf16[2,256,2304]{2,1,0:T(8,128)(2,1)} %all-gather.2.cloned.1.call-done) | copy-start | bytes 7077892
  205.8 1.9 copy-start.4
  207.8 96.8 %copy-start.5 = (s32[256]{0:T(256)S(1)}, s32[256]{0:T(256)}, u32[]{:S(2)}) copy-start(s32[256]{0:T(256)} %param.7) | copy-start | bytes 3076
  305.7 1.9 copy-start.3
  305.8 1.9 copy-start.2
  309.7 216.2 %all-reduce.3.cloned.1.call-start = ((), (), s32[]{:S(2)}) async-start(), calls=%async_computation.3 | async-start | bytes 294912
Sparse Core Ops, SparseCore 0:
  63.1 43.1 all-gather.1
  309.8 60.2 reduce-scatter.2
  373.6 152.2 all-reduce.2
where the time goes:
time: 534 us
  waiting for transfers between devices  254 us (48%)
  blocking collectives  244 us (46%)
  between operations  14.5 us (3%)
  matrix products  13.5 us (3%)
    unnamed x4, waiting for transfers between devices  153 us
    psum x1, blocking collectives, local(): row_total = lax.psum(jnp.sum(exponent, axis=1), ('tok', 'voc'))  96.8 us
    psum x1, blocking collectives, local(): lax.psum(jnp.sum(probability * cap_tangent, axis=1), ('tok', 'voc'))  94.9 us
    reduce_scatter x1, waiting for transfers between devices, local(): lax.psum_scatter(probe_part + head_part, 'tok', scatter_dimension=0, tile...  58.5 us
    all_gather x1, blocking collectives, local(): features = lax.all_gather(stacked, 'voc', axis=2, tiled=True)  52.7 us
    all_gather x1, waiting for transfers between devices, local(): gathered = lax.all_gather(features, 'tok', axis=1, tiled=True)  42.7 us
  transfers between devices with their start and end apart: 3, of which 3 were waited for; matrix products, arithmetic and copies ran while one was open for 1% of the time, Pallas kernels for 0%

commit v1 on v0

--- a/solution.py
+++ b/solution.py
@@ -23,7 +23,7 @@
     cap_slope = 1.0 - capped * capped
     exponent = jnp.exp(softcap_value * capped)
     cap_tangent = cap_slope * tangent
-    row_total = lax.psum(jnp.sum(exponent, axis=1), ("tok", "voc"))
+    row_total = jnp.sum(lax.all_gather(jnp.sum(exponent, axis=1), ("tok", "voc")), axis=0)
     probability = exponent / row_total[:, None]
     mean_tangent = lax.psum(jnp.sum(probability * cap_tangent, axis=1), ("tok", "voc"))
     factor = 1.0 + 2.0 * zloss_weight * jnp.log(row_total)

time: 534 us -> 558 us (1.045)
  blocking collectives: 244 us -> 267 us
    all_gather x0 -> x1, blocking collectives: none -> 118 us  [local(): lax.all_gather(jnp.sum(exponent, axis=1), ('tok', 'voc'))]
    psum x1 -> x0, blocking collectives: 96.8 us -> none  [local(): row_total = lax.psum(jnp.sum(exponent, axis=1), ('tok', 'voc'))]
where the time goes in v1:
time: 558 us
  blocking collectives  267 us (48%)
  waiting for transfers between devices  254 us (46%)
  between operations  14.5 us (3%)
  matrix products  13.5 us (2%)
    unnamed x4, waiting for transfers between devices  153 us
    all_gather x1, blocking collectives, local(): lax.all_gather(jnp.sum(exponent, axis=1), ('tok', 'voc'))  118 us
    psum x1, blocking collectives, local(): lax.psum(jnp.sum(probability * cap_tangent, axis=1), ('tok', 'voc'))  96.4 us
    reduce_scatter x1, waiting for transfers between devices, local(): lax.psum_scatter(probe_part + head_part, 'tok', scatter_dimension=0, tile...  58.5 us
    all_gather x1, blocking collectives, local(): features = lax.all_gather(stacked, 'voc', axis=2, tiled=True)  52.7 us
    all_gather x1, waiting for transfers between devices, local(): gathered = lax.all_gather(features, 'tok', axis=1, tiled=True)  42.7 us
  transfers between devices with their start and end apart: 3, of which 3 were waited for; matrix products, arithmetic and copies ran while one was open for 1% of the time, Pallas kernels for 0%

profile of v1, /device:TPU:2, one launch (start us, length us, event | category | flops | bytes accessed | tf_op | source)
XLA Modules:
  0.0 557.9 jit_solution(14523745523806159616)
XLA Ops:
  7.2 0.0 copy-start
  7.2 0.0 all-gather.4.cloned.1.call-start
  7.2 0.8 pad_maximum_fusion
  8.0 0.1 copy.12
  8.1 52.7 %all_gather.12 = bf16[2,16,2304]{1,0,2:T(2,128)(2,1)S(1)} all-gather(bf16[2,16,72]{1,0,2:T(2,128)(2,1)S(1)} %copy.12), channel_id=1, replica_groups=mesh['tok'=16,'voc'=32] {'voc'}, dimensions={2}, use_global_device_ids=true | all-gather | bytes 152064 | tf_op jit(solution)/shard_map/all_gather | solution.py:14
  60.8 2.2 copy.13
  63.0 0.0 all-gather.4.cloned.1.call-update
  63.0 0.0 reduce-scatter.3.cloned.1.call-start
  63.1 0.6 iota_add_fusion
  63.7 42.7 %all-gather.4.cloned.1.call-done = bf16[2,256,2304]{2,1,0:T(8,128)(2,1)} async-done(((bf16[2,16,2304]{2,1,0:T(8,128)(2,1)}), bf16[2,256,2304]{2,1,0:T(8,128)(2,1)}) %all-gather.4.cloned.1.call-update) | async-done | bytes 2359312 | tf_op jit(solution)/shard_map/all_gather | solution.py:15
  106.4 0.0 copy-done
  106.4 0.0 copy-start.1
  106.4 2.7 fusion.8
  109.1 117.8 %all-gather.1 = f32[512,1,256]{2,1,0:T(1,128)} all-gather(f32[1,1,256]{2,1,0:T(1,128)S(1)} %bitcast.35), channel_id=2, replica_groups=mesh['tok'=16,'voc'=32] {'tok','voc'}, dimensions={0}, use_global_device_ids=true | all-gather | bytes 525312 | tf_op jit(solution)/shard_map/all_gather | solution.py:26
  226.8 1.6 reduce_sum.28
  228.4 0.0 copy-done.1
  228.4 0.0 copy-start.4
  228.4 1.9 fusion.3
  230.4 0.0 copy-done.4
  230.4 0.0 copy-start.5
  230.4 1.8 multiply_reduce_fusion
  232.2 96.4 %psum.7 = f32[256]{0:T(256)S(1)} all-reduce(f32[256]{0:T(256)} %get-tuple-element.6), channel_id=1, replica_groups=mesh['tok'=16,'voc'=32] {'tok','voc'}, use_global_device_ids=true, to_apply=%region_3.0 | all-reduce | flops 256 | bytes 2048 | tf_op jit(solution)/shard_map/psum | solution.py:28
  328.6 0.0 copy-done.5
  328.6 1.2 add_convert_fusion
  329.8 0.0 copy-start.3
  329.8 0.0 copy-start.2
  329.8 1.9 fusion.10
  331.7 0.0 copy-done.3
  331.7 0.0 copy-done.2
  331.8 2.0 convolution_add_fusion
  333.7 0.0 reduce-scatter.3.cloned.1.call-update
  333.7 0.0 all-reduce.3.cloned.1.call-start
  333.8 1.3 dynamic-slice
  335.7 58.5 %reduce-scatter.3.cloned.1.call-done = f32[16,2304]{1,0:T(8,128)} async-done(((f32[256,2304]{1,0:T(8,128)}), f32[16,2304]{1,0:T(8,128)}) %reduce-scatter.3.cloned.1.call-update) | async-done | bytes 147472 | tf_op jit(solution)/shard_map/reduce_scatter | solution.py:50
  394.2 0.0 all-reduce.3.cloned.1.call-update
  394.2 3.2 convolution_bitcast_fusion
  397.4 152.5 %all-reduce.3.cloned.1.call-done = f32[16,2304]{1,0:T(8,128)} async-done(((f32[16,2304]{1,0:T(8,128)}), f32[16,2304]{1,0:T(8,128)}) %all-reduce.3.cloned.1.call-update) | async-done | bytes 147472
  550.0 1.4 constant_dynamic-slice_fusion
  (2 shorter events, 0.0 us)
Async XLA Ops:
  7.2 99.2 %copy-start = (bf16[2304,256]{1,0:T(8,128)(2,1)S(1)}, bf16[2304,256]{1,0:T(8,128)(2,1)}, u32[]{:S(2)}) copy-start(bf16[2304,256]{1,0:T(8,128)(2,1)} %param.6) | copy-start | bytes 3538948
  7.2 99.2 %all-gather.4.cloned.1.call-start = ((), (), s32[]{:S(2)}) async-start(), calls=%async_computation.1 | async-start | bytes 2506752 | tf_op jit(solution)/shard_map/all_gather | solution.py:15
  63.0 331.2 %reduce-scatter.3.cloned.1.call-start = ((), (), s32[]{:S(2)}) async-start(), calls=%async_computation.2 | async-start | bytes 2506752 | tf_op jit(solution)/shard_map/reduce_scatter | solution.py:50
  106.4 122.1 %copy-start.1 = (bf16[2,256,2304]{2,1,0:T(8,128)(2,1)S(1)}, bf16[2,256,2304]{2,1,0:T(8,128)(2,1)}, u32[]{:S(2)}) copy-start(bf16[2,256,2304]{2,1,0:T(8,128)(2,1)} %all-gather.4.cloned.1.call-done) | copy-start | bytes 7077892
  228.4 1.9 copy-start.4
  230.4 98.2 %copy-start.5 = (s32[256]{0:T(256)S(1)}, s32[256]{0:T(256)}, u32[]{:S(2)}) copy-start(s32[256]{0:T(256)} %param.7) | copy-start | bytes 3076
  329.8 1.9 copy-start.3
  329.8 1.9 copy-start.2
  333.7 216.2 %all-reduce.3.cloned.1.call-start = ((), (), s32[]{:S(2)}) async-start(), calls=%async_computation.3 | async-start | bytes 294912
Sparse Core Ops, SparseCore 0:
  63.1 43.1 all-gather.3
  333.9 60.2 reduce-scatter.2
  397.7 152.2 all-reduce.2
